TPU v7x, 32 devices: a whole 2x2x4 slice. The times are simulated.
32 devices in a mesh: row: 8 (over z, core), col: 4 (over y, x).
Axes of the slice: x: 2, y: 2, z: 4, core: 2. Of those that a mesh axis runs over, the one named last changes fastest.
Arguments:
- pivot_inverse: float32 [1024, 1024], P('row'), may hold values from -1 to 2, as said below
- panel: float32 [16, 1024, 1024], P('row', 'col'), may hold values from -1 to 1
- trailing: float32 [160, 1024, 1024], P('row', None, 'col'), may hold values from -6 to 6
- tile_list: int32 [160, 2], P('row'), may hold values from -1 to 15, as said below
Outputs:
- solved_panel: float32 [16, 1024, 1024], P('row', 'col')
- updated: float32 [160, 1024, 1024], P('row', None, 'col')
Inputs may be any that keep to these rules, and one draw needn't show every extreme that they name: `pivot_inverse`: lower triangular, diagonal between 0.5 and 2. `tile_list`: slots t of group g are g * 20 to g * 20 + 19. Column 0 lies in 0 to 1; column 1 is a panel tile or -1 for an empty slot. The live slots of a group come first and name distinct pairs; each group in the first half of the groups holds exactly 6 live slots, each in the second half exactly 20. Empty slots hold 0 in column 0.
All inputs are finite; a program needn't handle non-finite values.
Results may differ from a plain program's by a relative error of at most 0.00007.
Values sent between devices are 32-bit elements; how exact they have to be, the bound alone decides.
A program may use at most 128 MiB of HBM per device.

v0:
```python
import functools

import jax
import jax.numpy as jnp
from jax import lax
from jax.experimental import pallas as pl
from jax.experimental.pallas import tpu as pltpu
from jax.sharding import PartitionSpec as P

MESH = pl.DeviceIdType.MESH
LIGHT = 6
CHUNKS = 4
f32, bf16 = jnp.float32, jnp.bfloat16


def halves(x):
    hi = x.astype(bf16)
    return hi, (x - hi.astype(f32)).astype(bf16)


def dot_nt(a, b):
    return lax.dot_general(a, b, (((1,), (1,)), ((), ())), preferred_element_type=f32)


def dot_nn(a, b):
    return lax.dot_general(a, b, (((1,), (0,)), ((), ())), preferred_element_type=f32)


def table(index, values):
    found = jnp.int32(0)
    for at, value in enumerate(values):
        found = jnp.where(index == at, jnp.int32(value), found)
    return found


def kernel(rows, cols, pivot, panel, trailing, tiles, solved, updated,
           sl, q, factor, own_hi, own_lo, solved_buf, q3, acc,
           load_sem, in_sem, out_sem, solved_sem,
           lz_recv, lz_send, lr_recv, lr_send, ls_recv, ls_send,
           row_recv, row_send, sib_recv, sib_send, q_recv, q_send):
    chips = rows // 2
    pan, height, order = panel.shape
    slots = trailing.shape[0]
    kc = order // CHUNKS
    far = cols // 2
    rest = 3 if chips > 3 else chips
    ring = [i ^ (i >> 1) for i in range(cols)]
    where_in = [ring.index(i) for i in range(cols)]

    row, col = lax.axis_index("row"), lax.axis_index("col")
    chip, core = lax.div(row, 2), lax.rem(row, 2)
    spot = table(col, where_in)

    def ring_col(step):
        return table(lax.rem(spot + step + cols, cols), ring)

    above, below = (row + 2, col), (row - 2, col)
    sibling = (chip * 2 + 1 - core, col)
    ahead, behind = (row, ring_col(1)), (row, ring_col(-1))
    has_above, has_below = chip < chips - 1, chip > 0
    live = jnp.where(row < rows // 2, jnp.int32(min(LIGHT, slots)), jnp.int32(slots))

    def own_panel(c):
        return pltpu.make_async_copy(
            panel.at[:, :, pl.ds(c * kc, kc)], sl[c].at[pl.ds(row * pan, pan)], load_sem.at[c])

    share = pivot.shape[0] // cols
    own_factor = pltpu.make_async_copy(
        pivot.at[pl.ds(pl.multiple_of(col * share, share), share)], factor.at[core, col, chip], load_sem.at[CHUNKS])
    own_factor.start()
    for c in range(CHUNKS):
        own_panel(c).start()

    def slot_in(t):
        return pltpu.make_async_copy(trailing.at[t], acc.at[t], in_sem.at[t])

    def slot_out(t):
        return pltpu.make_async_copy(acc.at[t], updated.at[t], out_sem.at[t])

    def over(lo, hi, act):
        def body(t, carry):
            act(t)
            return carry
        lax.fori_loop(lo, hi, body, 0)

    barrier = pltpu.get_barrier_semaphore()
    for other in (sibling, ahead, behind):
        pl.semaphore_signal(barrier, inc=1, device_id=other, device_id_type=MESH)

    @pl.when(has_above)
    def _():
        pl.semaphore_signal(barrier, inc=1, device_id=above, device_id_type=MESH)

    @pl.when(has_below)
    def _():
        pl.semaphore_signal(barrier, inc=1, device_id=below, device_id_type=MESH)

    pl.semaphore_wait(barrier, 3 + jnp.where(has_above, 1, 0) + jnp.where(has_below, 1, 0))

    def remote(ref, send, recv, device):
        return pltpu.make_async_remote_copy(
            src_ref=ref, dst_ref=ref, send_sem=send, recv_sem=recv, device_id=device, device_id_type=MESH)

    def factor_line(up, src):
        return remote(factor.at[core, col, src], lz_send.at[0 if up else 1, src], lz_recv.at[src], above if up else below)

    hc = chips // 2

    def factor_part(side, at, h):
        return factor.at[side, at, pl.ds(h * hc, hc)]

    def factor_ring(fwd, at, h):
        return remote(factor_part(core, at, h), lr_send.at[0 if fwd else 1, at, h], lr_recv.at[at, h], ahead if fwd else behind)

    def factor_sib(side, at, h):
        return remote(factor_part(side, at, h), ls_send.at[at, h], ls_recv.at[at, h], sibling)

    def slices_of(c, src, side):
        return sl[c].at[pl.ds((src * 2 + side) * pan, pan)]

    def row_line(c, up, src):
        return remote(slices_of(c, src, core), row_send.at[c, 0 if up else 1, src], row_recv.at[c, src], above if up else below)

    def row_sib(c, src, side):
        return remote(slices_of(c, src, side), sib_send.at[c, src], sib_recv.at[c, src], sibling)

    def q_ring(c, fwd, at, h):
        return remote(q[c].at[h, at], q_send.at[c, 0 if fwd else 1, at, h], q_recv.at[c, at, h], ahead if fwd else behind)

    def line_own(make):
        @pl.when(has_above)
        def _():
            make(True, chip).start()

        @pl.when(has_below)
        def _():
            make(False, chip).start()

    def line_event(make, d, also):
        @pl.when(chip - d >= 0)
        def _():
            make(True, chip - d).wait_recv()

            @pl.when(has_above)
            def _():
                make(True, chip - d).start()
            also(chip - d)

        @pl.when(chip + d < chips)
        def _():
            make(False, chip + d).wait_recv()

            @pl.when(has_below)
            def _():
                make(False, chip + d).start()
            also(chip + d)

    def line_drain(make):
        @pl.when(has_above)
        def _():
            over(0, chip + 1, lambda src: make(True, src).wait_send())

        @pl.when(has_below)
        def _():
            over(chip, chips, lambda src: make(False, src).wait_send())

    def goes(d, fwd, h, count):
        return d < far or (d == far and (2 * h < count) == fwd)

    def ring_event(make, d, count, also):
        for h in range(count):
            for fwd in (True, False):
                if goes(d, fwd, h, count):
                    at = ring_col(-d if fwd else d)
                    if d > 0:
                        make(fwd, at, h).wait_recv()
                    if goes(d + 1, fwd, h, count):
                        make(fwd, at, h).start()
                    if d > 0:
                        also(at, h)

    def ring_drain(make, count):
        for d in range(far):
            for h in range(count):
                for fwd in (True, False):
                    if goes(d + 1, fwd, h, count):
                        make(fwd, ring_col(-d if fwd else d), h).wait_send()

    def row_own(c):
        line_own(functools.partial(row_line, c))
        row_sib(c, chip, core).start()

    def row_event(c, lo, hi):
        for d in range(lo, hi):
            line_event(functools.partial(row_line, c), d, lambda src: row_sib(c, src, core).start())

    def q_event(c, d):
        ring_event(functools.partial(q_ring, c), d, pan, lambda at, h: None)

    own_factor.wait()
    line_own(factor_line)
    own_panel(0).wait()
    row_own(0)
    over(0, slots, lambda t: slot_in(t).start())
    for c in range(1, CHUNKS):
        own_panel(c).wait()

    for c in range(CHUNKS):
        hi, lo = halves(sl[c][pl.ds(row * pan, pan)].reshape(pan * height, kc))
        own_hi[:, c * kc:(c + 1) * kc] = hi
        own_lo[:, c * kc:(c + 1) * kc] = lo

    for d in range(1, chips):
        line_event(factor_line, d, lambda src: None)
    row_own(1)

    def untouched(t):
        slot_in(t).wait()
        slot_out(t).start()

    over(live, slots, untouched)

    def pass_factor(at, h):
        factor_sib(core, at, h).start()

    ring_event(factor_ring, 0, 2, pass_factor)
    for h in range(2):
        pass_factor(col, h)
    row_event(0, 1, 2)
    ring_event(factor_ring, 1, 2, pass_factor)
    row_event(0, 2, rest)
    for d in range(2, far + 1):
        ring_event(factor_ring, d, 2, pass_factor)
    row_own(2)
    for at in range(cols):
        for h in range(2):
            factor_sib(1 - core, at, h).wait_recv()
    row_event(1, 1, 2)

    block = order // chips
    for b in range(chips):
        depth = min(order, -(-((b + 1) * block) // 128) * 128)
        l_hi, l_lo = halves(factor[:, :, b, :, :depth].reshape(block, depth))
        a_hi, a_lo = own_hi[:, :depth], own_lo[:, :depth]
        part = dot_nt(a_hi, l_hi) + (dot_nt(a_hi, l_lo) + dot_nt(a_lo, l_hi))
        solved_buf[:, :, b * block:(b + 1) * block] = part.reshape(pan, height, block)
    solved_copy = pltpu.make_async_copy(solved_buf, solved, solved_sem)
    for b in range(CHUNKS):
        hi, lo = halves(solved_buf[:, :, b * kc:(b + 1) * kc].reshape(pan * height, kc))
        own_hi[:, b * kc:(b + 1) * kc] = hi
        own_lo[:, b * kc:(b + 1) * kc] = lo
    solved_copy.start()

    for c in range(CHUNKS):
        first = (c * kc) // block
        span = pl.ds(c * kc, kc)
        l_rows = jnp.concatenate([factor[:, :, b, :, span].reshape(block, kc) for b in range(first, chips)], axis=0)
        l_hi, l_lo = halves(l_rows)
        s_hi, s_lo = own_hi[:, first * block:], own_lo[:, first * block:]
        part = dot_nn(s_hi, l_hi) + (dot_nn(s_hi, l_lo) + dot_nn(s_lo, l_hi))
        part = part.reshape(pan, height, kc)
        for h in range(pan):
            q[c][h, col] = part[h]
        q_event(c, 0)
        if c == 1:
            row_event(1, 2, rest)
    row_own(3)
    q_event(0, 1)

    def update(c, part, parts):
        def one(t):
            left = q3[tiles[t, 0]]
            r_hi, r_lo = halves(sl[c][tiles[t, 1]])
            right = jnp.concatenate([r_hi, r_lo, r_hi], axis=1)
            if c == 0:
                slot_in(t).wait()
            acc[t] = acc[t] - dot_nt(left, right)
            if c == CHUNKS - 1:
                slot_out(t).start()
        over(live * part // parts, live * (part + 1) // parts, one)

    for c in range(CHUNKS):
        for d in range(2, far + 1):
            q_event(c, d)
        if c + 1 < CHUNKS:
            q_event(c + 1, 1)
        for h in range(pan):
            hi, lo = halves(q[c][h].reshape(cols * height, kc))
            q3[h, :, 0:kc] = hi
            q3[h, :, kc:2 * kc] = hi
            q3[h, :, 2 * kc:3 * kc] = lo
        row_event(c, rest, chips)
        over(0, chips, lambda src: row_sib(c, src, 1 - core).wait_recv())
        update(c, 0, 2)
        if c + 2 < CHUNKS:
            row_event(c + 2, 1, 2)
        update(c, 1, 2)
        if c + 2 < CHUNKS:
            row_event(c + 2, 2, rest)

    line_drain(factor_line)
    ring_drain(factor_ring, 2)
    for at in range(cols):
        for h in range(2):
            factor_sib(core, at, h).wait_send()
    for c in range(CHUNKS):
        line_drain(functools.partial(row_line, c))
        over(0, chips, lambda src: row_sib(c, src, core).wait_send())
        ring_drain(functools.partial(q_ring, c), pan)
    solved_copy.wait()
    over(0, slots, lambda t: slot_out(t).wait())


def per_device(rows, cols, pivot_inverse, panel, trailing, tile_list):
    pan, height, order = panel.shape
    slots, _, width = trailing.shape
    chips, kc = rows // 2, order // CHUNKS
    share = pivot_inverse.shape[0] // cols
    dma = pltpu.SemaphoreType.DMA
    anywhere = pl.BlockSpec(memory_space=pl.ANY)
    return pl.pallas_call(
        functools.partial(kernel, rows, cols),
        out_shape=(
            jax.ShapeDtypeStruct(panel.shape, f32),
            jax.ShapeDtypeStruct(trailing.shape, f32),
        ),
        in_specs=[anywhere, anywhere, anywhere, pl.BlockSpec(memory_space=pltpu.SMEM)],
        out_specs=(anywhere, anywhere),
        scratch_shapes=[
            [pltpu.VMEM((rows * pan, height, kc), f32) for _ in range(CHUNKS)],
            [pltpu.VMEM((pan, cols, height, kc), f32) for _ in range(CHUNKS)],
            pltpu.VMEM((2, cols, chips, share, order), f32),
            pltpu.VMEM((pan * height, order), bf16),
            pltpu.VMEM((pan * height, order), bf16),
            pltpu.VMEM((pan, height, order), f32),
            pltpu.VMEM((pan, cols * height, 3 * kc), bf16),
            pltpu.VMEM((slots, order, width), f32),
            dma((CHUNKS + 1,)),
            dma((slots,)),
            dma((slots,)),
            dma(()),
            dma((chips,)),
            dma((2, chips)),
            dma((cols, 2)),
            dma((2, cols, 2)),
            dma((cols, 2)),
            dma((cols, 2)),
            dma((CHUNKS, chips)),
            dma((CHUNKS, 2, chips)),
            dma((CHUNKS, chips)),
            dma((CHUNKS, chips)),
            dma((CHUNKS, cols, pan)),
            dma((CHUNKS, 2, cols, pan)),
        ],
        compiler_params=pltpu.CompilerParams(
            collective_id=0, has_side_effects=True, vmem_limit_bytes=67043328
        ),
    )(pivot_inverse, panel, trailing, tile_list)


def solution(mesh):
    placed = (P("row", None), P("row", "col", None), P("row", None, "col"), P("row", None))
    return jax.shard_map(
        functools.partial(per_device, mesh.shape["row"], mesh.shape["col"]),
        mesh=mesh,
        in_specs=placed,
        out_specs=(P("row", "col", None), P("row", None, "col")),
        check_vma=False,
    )
```

profile of v0, /device:TPU:27, one launch (start us, length us, event | category | flops | bytes accessed | tf_op | source)
XLA Modules:
  0.0 198.7 jit_solution(1098380090137165582)
XLA Ops:
  0.6 1.4 copy.6.tiles
  2.0 177.8 %shard_map.59 = (f32[2,256,1024]{2,1,0:T(8,128)}, f32[20,1024,256]{2,1,0:T(8,128)}) custom-call(f32[128,1024]{1,0:T(8,128)} %pivot.1, f32[2,256,1024]{2,1,0:T(8,128)} %panel.1, f32[20,1024,256]{2,1,0:T(8,128)} %trailing.1, s32[20,2]{1,0:T(8,128)} %copy.6.tiles), custom_call_target="tpu_custom_call" | custom-call | tf_op jit(solution)/shard_map/pallas_call | solution.py:321
  179.8 3.2 %copy.9 = f32[2,256,1024]{2,1,0:T(8,128)} copy(f32[2,256,1024]{2,1,0:T(8,128)} %get-tuple-element.4) | data formatting | bytes 4194304
  182.9 15.8 %copy.10 = f32[20,1024,256]{2,1,0:T(8,128)} copy(f32[20,1024,256]{2,1,0:T(8,128)} %get-tuple-element.5) | data formatting | bytes 41943040
where the time goes:
time: 199 us
  Pallas kernels  178 us (89%)
  local copies, waits for them, and re-layouts  20.3 us (10%)
    pallas_call x1, Pallas kernels, per_device(): pl.pallas_call(functools.partial(kernel, rows, cols), out_shape=(jax.Shap...  178 us
    unnamed x3, local copies, waits for them, and re-layouts  20.3 us

commit v1 on v0

v1 whole, which is shorter than its diff:
```python
import functools

import jax
import jax.numpy as jnp
from jax import lax
from jax.experimental import pallas as pl
from jax.experimental.pallas import tpu as pltpu
from jax.sharding import PartitionSpec as P

MESH = pl.DeviceIdType.MESH
LIGHT = 6
CHUNKS = 4
STAGES = 4
PIECES = (4, 1, 1, 2)
f32, bf16 = jnp.float32, jnp.bfloat16


def halves(x):
    hi = x.astype(bf16)
    return hi, (x - hi.astype(f32)).astype(bf16)


def dot_nt(a, b):
    return lax.dot_general(a, b, (((1,), (1,)), ((), ())), preferred_element_type=f32)


def dot_nn(a, b):
    return lax.dot_general(a, b, (((1,), (0,)), ((), ())), preferred_element_type=f32)


def table(index, values):
    found = jnp.int32(0)
    for at, value in enumerate(values):
        found = jnp.where(index == at, jnp.int32(value), found)
    return found


def over(lo, hi, act):
    def body(t, carry):
        act(t)
        return carry
    lax.fori_loop(lo, hi, body, 0)


def live_slots(row, rows, slots):
    return jnp.where(row < rows // 2, jnp.int32(min(LIGHT, slots)), jnp.int32(slots))


def gather_kernel(rows, cols, pivot, panel, trailing, tiles,
                  solved_buf, acc, q3_last, sl_last,
                  sl, q, factor, own_hi, own_lo, q3,
                  load_sem, in_sem,
                  lz_recv, lz_send, lr_recv, lr_send, ls_recv, ls_send,
                  row_recv, row_send, sib_recv, sib_send, q_recv, q_send):
    chips = rows // 2
    pan, height, order = panel.shape
    slots = trailing.shape[0]
    kc = order // CHUNKS
    block = order // chips
    far = cols // 2
    sl = [*sl, sl_last]
    ring = [i ^ (i >> 1) for i in range(cols)]
    where_in = [ring.index(i) for i in range(cols)]

    row, col = lax.axis_index("row"), lax.axis_index("col")
    chip, core = lax.div(row, 2), lax.rem(row, 2)
    spot = table(col, where_in)

    def ring_col(step):
        return table(lax.rem(spot + step + cols, cols), ring)

    above, below = (row + 2, col), (row - 2, col)
    sibling = (chip * 2 + 1 - core, col)
    ahead, behind = (row, ring_col(1)), (row, ring_col(-1))
    has_above, has_below = chip < chips - 1, chip > 0
    live = live_slots(row, rows, slots)

    def own_panel(c):
        return pltpu.make_async_copy(
            panel.at[:, :, pl.ds(c * kc, kc)], sl[c].at[pl.ds(row * pan, pan)], load_sem.at[c])

    share = pivot.shape[0] // cols
    own_factor = pltpu.make_async_copy(
        pivot.at[pl.ds(pl.multiple_of(col * share, share), share)], factor.at[core, col, chip], load_sem.at[CHUNKS])
    own_factor.start()
    for c in range(CHUNKS):
        own_panel(c).start()

    def slot_in(t):
        return pltpu.make_async_copy(trailing.at[t], acc.at[t], in_sem.at[t])

    barrier = pltpu.get_barrier_semaphore()
    for other in (sibling, ahead, behind):
        pl.semaphore_signal(barrier, inc=1, device_id=other, device_id_type=MESH)

    @pl.when(has_above)
    def _():
        pl.semaphore_signal(barrier, inc=1, device_id=above, device_id_type=MESH)

    @pl.when(has_below)
    def _():
        pl.semaphore_signal(barrier, inc=1, device_id=below, device_id_type=MESH)

    pl.semaphore_wait(barrier, 3 + jnp.where(has_above, 1, 0) + jnp.where(has_below, 1, 0))

    def remote(ref, send, recv, device):
        return pltpu.make_async_remote_copy(
            src_ref=ref, dst_ref=ref, send_sem=send, recv_sem=recv, device_id=device, device_id_type=MESH)

    def factor_part(side, at, src):
        depth = -(-((src + 1) * block) // kc) * kc
        return factor.at[side, at, src, :, pl.ds(0, depth)]

    def factor_line(up, src):
        return remote(factor_part(core, col, src), lz_send.at[0 if up else 1, src], lz_recv.at[src], above if up else below)

    def factor_ring(fwd, at, src):
        return remote(factor_part(core, at, src), lr_send.at[0 if fwd else 1, at, src], lr_recv.at[at, src], ahead if fwd else behind)

    def factor_sib(side, at, src):
        return remote(factor_part(side, at, src), ls_send.at[at, src], ls_recv.at[at, src], sibling)

    def piece(c, src, side, i):
        first = (src * 2 + side) * pan
        count = PIECES[c]
        if count <= pan:
            return sl[c].at[pl.ds(first + i * (pan // count), pan // count)]
        splits = count // pan
        return sl[c].at[first + i // splits, pl.ds((i % splits) * (height // splits), height // splits)]

    def row_line(c, i, up, src):
        return remote(piece(c, src, core, i), row_send.at[c, i, 0 if up else 1, src], row_recv.at[c, i, src], above if up else below)

    def row_sib(c, i, src, side):
        return remote(piece(c, src, side, i), sib_send.at[c, i, src], sib_recv.at[c, i, src], sibling)

    def q_ring(c, fwd, at, h):
        return remote(q[c].at[h, at], q_send.at[c, 0 if fwd else 1, at, h], q_recv.at[c, at, h], ahead if fwd else behind)

    def goes(d, fwd, h):
        return d < far or (d == far and (h % 2 == 0) == fwd)

    def factor_own():
        for s in range(chips):
            @pl.when(chip == s)
            def _():
                @pl.when(has_above)
                def _():
                    factor_line(True, s).start()

                @pl.when(has_below)
                def _():
                    factor_line(False, s).start()
                factor_spread(s)

    def factor_spread(s):
        for fwd in (True, False):
            if goes(1, fwd, s):
                factor_ring(fwd, col, s).start()
        factor_sib(core, col, s).start()

    def factor_event(d):
        for s in range(chips):
            @pl.when(chip - d == s)
            def _():
                factor_line(True, s).wait_recv()

                @pl.when(has_above)
                def _():
                    factor_line(True, s).start()
                factor_spread(s)

            @pl.when(chip + d == s)
            def _():
                factor_line(False, s).wait_recv()

                @pl.when(has_below)
                def _():
                    factor_line(False, s).start()
                factor_spread(s)

    def factor_ring_event(d):
        for s in range(chips):
            for fwd in (True, False):
                if goes(d, fwd, s):
                    at = ring_col(-d if fwd else d)
                    factor_ring(fwd, at, s).wait_recv()
                    if goes(d + 1, fwd, s):
                        factor_ring(fwd, at, s).start()
                    factor_sib(core, at, s).start()

    def factor_drain():
        for s in range(chips):
            @pl.when(has_above & (chip >= s))
            def _():
                factor_line(True, s).wait_send()

            @pl.when(has_below & (chip <= s))
            def _():
                factor_line(False, s).wait_send()
            for at in range(cols):
                factor_sib(core, at, s).wait_send()
            for d in range(far):
                for fwd in (True, False):
                    if goes(d + 1, fwd, s):
                        factor_ring(fwd, ring_col(-d if fwd else d), s).wait_send()

    def row_own(c, i):
        @pl.when(has_above)
        def _():
            row_line(c, i, True, chip).start()

        @pl.when(has_below)
        def _():
            row_line(c, i, False, chip).start()
        row_sib(c, i, chip, core).start()

    def row_event(c, d):
        for i in range(PIECES[c]):
            @pl.when(chip - d >= 0)
            def _():
                row_line(c, i, True, chip - d).wait_recv()

                @pl.when(has_above)
                def _():
                    row_line(c, i, True, chip - d).start()
                row_sib(c, i, chip - d, core).start()

            @pl.when(chip + d < chips)
            def _():
                row_line(c, i, False, chip + d).wait_recv()

                @pl.when(has_below)
                def _():
                    row_line(c, i, False, chip + d).start()
                row_sib(c, i, chip + d, core).start()

    def row_drain(c):
        for i in range(PIECES[c]):
            @pl.when(has_above)
            def _():
                over(0, chip + 1, lambda src: row_line(c, i, True, src).wait_send())

            @pl.when(has_below)
            def _():
                over(chip, chips, lambda src: row_line(c, i, False, src).wait_send())
            over(0, chips, lambda src: row_sib(c, i, src, core).wait_send())

    def q_event(c, d):
        for h in range(pan):
            for fwd in (True, False):
                if goes(d, fwd, h):
                    at = ring_col(-d if fwd else d)
                    if d > 0:
                        q_ring(c, fwd, at, h).wait_recv()
                    if goes(d + 1, fwd, h):
                        q_ring(c, fwd, at, h).start()

    def q_drain(c):
        for d in range(far):
            for h in range(pan):
                for fwd in (True, False):
                    if goes(d + 1, fwd, h):
                        q_ring(c, fwd, ring_col(-d if fwd else d), h).wait_send()

    own_factor.wait()
    factor_own()
    own_panel(0).wait()
    sent = 0
    for d in range(1, chips):
        if sent < PIECES[0]:
            row_own(0, sent)
            sent += 1
        factor_event(d)
    for i in range(sent, PIECES[0]):
        row_own(0, i)
    for c in range(1, CHUNKS):
        own_panel(c).wait()
        for i in range(PIECES[c]):
            row_own(c, i)
    over(0, slots, lambda t: slot_in(t).start())

    for c in range(CHUNKS):
        hi, lo = halves(sl[c][pl.ds(row * pan, pan)].reshape(pan * height, kc))
        own_hi[:, c * kc:(c + 1) * kc] = hi
        own_lo[:, c * kc:(c + 1) * kc] = lo

    for d in range(1, far + 1):
        factor_ring_event(d)
    for s in range(chips):
        for at in range(cols):
            factor_sib(1 - core, at, s).wait_recv()

    for b in range(chips):
        depth = min(order, -(-((b + 1) * block) // 128) * 128)
        l_hi, l_lo = halves(factor[:, :, b, :, :depth].reshape(block, depth))
        a_hi, a_lo = own_hi[:, :depth], own_lo[:, :depth]
        part = dot_nt(a_hi, l_hi) + (dot_nt(a_hi, l_lo) + dot_nt(a_lo, l_hi))
        solved_buf[:, :, b * block:(b + 1) * block] = part.reshape(pan, height, block)
    for b in range(CHUNKS):
        hi, lo = halves(solved_buf[:, :, b * kc:(b + 1) * kc].reshape(pan * height, kc))
        own_hi[:, b * kc:(b + 1) * kc] = hi
        own_lo[:, b * kc:(b + 1) * kc] = lo

    for c in range(CHUNKS):
        first = (c * kc) // block
        span = pl.ds(c * kc, kc)
        l_rows = jnp.concatenate([factor[:, :, b, :, span].reshape(block, kc) for b in range(first, chips)], axis=0)
        l_hi, l_lo = halves(l_rows)
        s_hi, s_lo = own_hi[:, first * block:], own_lo[:, first * block:]
        part = dot_nn(s_hi, l_hi) + (dot_nn(s_hi, l_lo) + dot_nn(s_lo, l_hi))
        part = part.reshape(pan, height, kc)
        for h in range(pan):
            q[c][h, col] = part[h]
        q_event(c, 0)

    for c in range(CHUNKS):
        row_event(c, 1)
        if c > 0:
            for d in range(1, far):
                q_event(c - 1, d)
    for d in range(2, chips - 1):
        for c in range(CHUNKS):
            row_event(c, d)
            if d == 2 and c == 0:
                for e in range(1, far):
                    q_event(CHUNKS - 1, e)
    for c in range(CHUNKS):
        q_event(c, far)

    over(0, slots, lambda t: slot_in(t).wait())

    def update(c):
        def one(t):
            left = q3[tiles[0, t]]
            r_hi, r_lo = halves(sl[c][tiles[1, t]])
            right = jnp.concatenate([r_hi, r_lo, r_hi], axis=1)
            acc[t] = acc[t] - dot_nt(left, right)
        over(0, live, one)

    for c in range(CHUNKS):
        into = q3 if c < CHUNKS - 1 else q3_last
        for h in range(pan):
            hi, lo = halves(q[c][h].reshape(cols * height, kc))
            into[h, :, 0:kc] = hi
            into[h, :, kc:2 * kc] = hi
            into[h, :, 2 * kc:3 * kc] = lo
        row_event(c, chips - 1)
        for i in range(PIECES[c]):
            over(0, chips, lambda src: row_sib(c, i, src, 1 - core).wait_recv())
        if c < CHUNKS - 1:
            update(c)

    factor_drain()
    for c in range(CHUNKS):
        row_drain(c)
        q_drain(c)


def finish_kernel(rows, solved_buf, acc, q3, right_tiles, tiles, solved, updated,
                  solved_stage, stage, solved_sem, out_sem):
    slots = acc.shape[0]
    live = live_slots(lax.axis_index("row"), rows, slots)
    solved_copy = pltpu.make_async_copy(solved_stage, solved, solved_sem)

    def slot_out(t):
        at = lax.rem(t, STAGES)
        return pltpu.make_async_copy(stage.at[at], updated.at[t], out_sem.at[at])

    def staged(value):
        def one(t):
            @pl.when(t >= STAGES)
            def _():
                slot_out(t - STAGES).wait()

            stage[lax.rem(t, STAGES)] = value(t)
            slot_out(t).start()
        return one

    def touched(t):
        r_hi, r_lo = halves(right_tiles[tiles[1, t]])
        right = jnp.concatenate([r_hi, r_lo, r_hi], axis=1)
        return acc[t] - dot_nt(q3[tiles[0, t]], right)

    over(0, live, staged(touched))
    over(live, slots, staged(lambda t: acc[t]))
    solved_stage[...] = solved_buf[...]
    solved_copy.start()
    over(slots - STAGES, slots, lambda t: slot_out(t).wait())
    solved_copy.wait()


def per_device(rows, cols, pivot_inverse, panel, trailing, tile_list):
    pan, height, order = panel.shape
    slots, _, width = trailing.shape
    chips, kc = rows // 2, order // CHUNKS
    share = pivot_inverse.shape[0] // cols
    most = max(PIECES)
    dma = pltpu.SemaphoreType.DMA
    anywhere = pl.BlockSpec(memory_space=pl.ANY)
    vector = pl.BlockSpec(memory_space=pltpu.VMEM)
    scalar = pl.BlockSpec(memory_space=pltpu.SMEM)
    tiles = tile_list.T
    carried = pl.pallas_call(
        functools.partial(gather_kernel, rows, cols),
        out_shape=(
            pltpu.VMEM(panel.shape, f32),
            pltpu.VMEM(trailing.shape, f32),
            pltpu.VMEM((pan, cols * height, 3 * kc), bf16),
            pltpu.VMEM((rows * pan, height, kc), f32),
        ),
        in_specs=[anywhere, anywhere, anywhere, scalar],
        out_specs=(vector,) * 4,
        scratch_shapes=[
            [pltpu.VMEM((rows * pan, height, kc), f32) for _ in range(CHUNKS - 1)],
            [pltpu.VMEM((pan, cols, height, kc), f32) for _ in range(CHUNKS)],
            pltpu.VMEM((2, cols, chips, share, order), f32),
            pltpu.VMEM((pan * height, order), bf16),
            pltpu.VMEM((pan * height, order), bf16),
            pltpu.VMEM((pan, cols * height, 3 * kc), bf16),
            dma((CHUNKS + 1,)),
            dma((slots,)),
            dma((chips,)),
            dma((2, chips)),
            dma((cols, chips)),
            dma((2, cols, chips)),
            dma((cols, chips)),
            dma((cols, chips)),
            dma((CHUNKS, most, chips)),
            dma((CHUNKS, most, 2, chips)),
            dma((CHUNKS, most, chips)),
            dma((CHUNKS, most, chips)),
            dma((CHUNKS, cols, pan)),
            dma((CHUNKS, 2, cols, pan)),
        ],
        compiler_params=pltpu.CompilerParams(
            collective_id=0, has_side_effects=True, vmem_limit_bytes=34 * 1024 * 1024
        ),
    )(pivot_inverse, panel, trailing, tiles)
    carried = [pltpu.with_memory_space_constraint(x, pltpu.VMEM) for x in carried]
    return pl.pallas_call(
        functools.partial(finish_kernel, rows),
        out_shape=(
            jax.ShapeDtypeStruct(panel.shape, f32),
            jax.ShapeDtypeStruct(trailing.shape, f32),
        ),
        in_specs=[vector, vector, vector, vector, scalar],
        out_specs=(anywhere, anywhere),
        scratch_shapes=[
            pltpu.VMEM(panel.shape, f32),
            pltpu.VMEM((STAGES, order, width), f32),
            dma(()),
            dma((STAGES,)),
        ],
        compiler_params=pltpu.CompilerParams(vmem_limit_bytes=34 * 1024 * 1024),
    )(*carried, tiles)


def solution(mesh):
    placed = (P("row", None), P("row", "col", None), P("row", None, "col"), P("row", None))
    return jax.shard_map(
        functools.partial(per_device, mesh.shape["row"], mesh.shape["col"]),
        mesh=mesh,
        in_specs=placed,
        out_specs=(P("row", "col", None), P("row", None, "col")),
        check_vma=False,
    )
```

time: 199 us -> 174 us (0.87)
  local copies, waits for them, and re-layouts: 20.3 us -> 0 us
  Pallas kernels: 178 us -> 173 us
    unnamed x3 -> x0, local copies, waits for them, and re-layouts: 20.3 us -> none
    pallas_call x1 -> x2, Pallas kernels: 178 us -> 173 us  [the longest x1 159 us: per_device(): pl.pallas_call(functools.partial(gather_kernel, rows, cols), out_shape=(p...]
where the time goes in v1:
time: 174 us
  Pallas kernels  173 us (99%)
    pallas_call x1, Pallas kernels, per_device(): pl.pallas_call(functools.partial(gather_kernel, rows, cols), out_shape=(p...  159 us
    pallas_call x1, Pallas kernels, per_device(): pl.pallas_call(functools.partial(finish_kernel, rows), out_shape=(jax.Sha...  14.7 us

profile of v1, /device:TPU:27, one launch (start us, length us, event | category | flops | bytes accessed | tf_op | source)
XLA Modules:
  0.0 174.0 jit_solution(13744286316820929365)
XLA Ops:
  0.6 158.6 %shard_map.59 = (f32[2,256,1024]{2,1,0:T(8,128)S(1)}, f32[20,1024,256]{2,1,0:T(8,128)S(1)}, bf16[2,1024,768]{2,1,0:T(8,128)(2,1)S(1)}, f32[16,256,256]{2,1,0:T(8,128)S(1)}) custom-call(f32[128,1024]{1,0:T(8,128)} %pivot.1, f32[2,256,1024]{2,1,0:T(8,128)} %panel.1, f32[20,1024,256]{2,1,0:T(8,128)} %trailing.1, s32[2,20]{1,0:T(2,128)} %bitcast.1), custom_call_target="tpu_custom_call" | custom-call | tf_op jit(solution)/shard_map/pallas_call | solution.py:404
  159.3 14.7 %shard_map.60 = (f32[2,256,1024]{2,1,0:T(8,128)}, f32[20,1024,256]{2,1,0:T(8,128)}) custom-call(f32[2,256,1024]{2,1,0:T(8,128)S(1)} %get-tuple-element.6.solved_buf, f32[20,1024,256]{2,1,0:T(8,128)S(1)} %get-tuple-element.7.acc, bf16[2,1024,768]{2,1,0:T(8,128)(2,1)S(1)} %get-tuple-element.8.q3, f32[16,256,256]{2,1,0:T(8,128)S(1)} %get-tuple-element.9.right_tiles, ...), custom_call_target="tpu_custom_call" | custom-call | tf_op jit(solution)/shard_map/pallas_call | solution.py:441

commit v2 on v1

--- a/solution.py
+++ b/solution.py
@@ -9,9 +9,10 @@
 
 MESH = pl.DeviceIdType.MESH
 LIGHT = 6
-CHUNKS = 4
+PARTS = (2, 2, 2, 1, 1)
+PIECES = (4, 1, 1, 1, 2)
+CHUNKS = len(PARTS)
 STAGES = 4
-PIECES = (4, 1, 1, 2)
 f32, bf16 = jnp.float32, jnp.bfloat16
 
 
@@ -33,6 +34,11 @@
     for at, value in enumerate(values):
         found = jnp.where(index == at, jnp.int32(value), found)
     return found
+
+
+def chunk_spans(order):
+    unit = order // sum(PARTS)
+    return [(sum(PARTS[:c]) * unit, PARTS[c] * unit) for c in range(CHUNKS)]
 
 
 def over(lo, hi, act):
@@ -55,7 +61,7 @@
     chips = rows // 2
     pan, height, order = panel.shape
     slots = trailing.shape[0]
-    kc = order // CHUNKS
+    spans = chunk_spans(order)
     block = order // chips
     far = cols // 2
     sl = [*sl, sl_last]
@@ -77,7 +83,7 @@
 
     def own_panel(c):
         return pltpu.make_async_copy(
-            panel.at[:, :, pl.ds(c * kc, kc)], sl[c].at[pl.ds(row * pan, pan)], load_sem.at[c])
+            panel.at[:, :, pl.ds(*spans[c])], sl[c].at[pl.ds(row * pan, pan)], load_sem.at[c])
 
     share = pivot.shape[0] // cols
     own_factor = pltpu.make_async_copy(
@@ -107,8 +113,11 @@
         return pltpu.make_async_remote_copy(
             src_ref=ref, dst_ref=ref, send_sem=send, recv_sem=recv, device_id=device, device_id_type=MESH)
 
+    def reach(b):
+        return min(at + kc for at, kc in spans if at + kc >= (b + 1) * block)
+
     def factor_part(side, at, src):
-        depth = -(-((src + 1) * block) // kc) * kc
+        depth = reach(src)
         return factor.at[side, at, src, :, pl.ds(0, depth)]
 
     def factor_line(up, src):
@@ -215,23 +224,19 @@
             row_line(c, i, False, chip).start()
         row_sib(c, i, chip, core).start()
 
-    def row_event(c, d):
+    def row_event(c, d, relay):
         for i in range(PIECES[c]):
-            @pl.when(chip - d >= 0)
+            @pl.when((chip - d >= 0) & (has_above if relay else ~has_above))
             def _():
                 row_line(c, i, True, chip - d).wait_recv()
-
-                @pl.when(has_above)
-                def _():
+                if relay:
                     row_line(c, i, True, chip - d).start()
                 row_sib(c, i, chip - d, core).start()
 
-            @pl.when(chip + d < chips)
+            @pl.when((chip + d < chips) & (has_below if relay else ~has_below))
             def _():
                 row_line(c, i, False, chip + d).wait_recv()
-
-                @pl.when(has_below)
-                def _():
+                if relay:
                     row_line(c, i, False, chip + d).start()
                 row_sib(c, i, chip + d, core).start()
 
@@ -274,16 +279,21 @@
         factor_event(d)
     for i in range(sent, PIECES[0]):
         row_own(0, i)
+
+    def own_send(c):
+        for i in range(PIECES[c]):
+            row_own(c, i)
+
     for c in range(1, CHUNKS):
         own_panel(c).wait()
-        for i in range(PIECES[c]):
-            row_own(c, i)
+        if c < 3:
+            own_send(c)
     over(0, slots, lambda t: slot_in(t).start())
 
-    for c in range(CHUNKS):
+    for c, (at, kc) in enumerate(spans):
         hi, lo = halves(sl[c][pl.ds(row * pan, pan)].reshape(pan * height, kc))
-        own_hi[:, c * kc:(c + 1) * kc] = hi
-        own_lo[:, c * kc:(c + 1) * kc] = lo
+        own_hi[:, at:at + kc] = hi
+        own_lo[:, at:at + kc] = lo
 
     for d in range(1, far + 1):
         factor_ring_event(d)
@@ -292,20 +302,19 @@
             factor_sib(1 - core, at, s).wait_recv()
 
     for b in range(chips):
-        depth = min(order, -(-((b + 1) * block) // 128) * 128)
+        depth = reach(b)
         l_hi, l_lo = halves(factor[:, :, b, :, :depth].reshape(block, depth))
         a_hi, a_lo = own_hi[:, :depth], own_lo[:, :depth]
         part = dot_nt(a_hi, l_hi) + (dot_nt(a_hi, l_lo) + dot_nt(a_lo, l_hi))
         solved_buf[:, :, b * block:(b + 1) * block] = part.reshape(pan, height, block)
-    for b in range(CHUNKS):
-        hi, lo = halves(solved_buf[:, :, b * kc:(b + 1) * kc].reshape(pan * height, kc))
-        own_hi[:, b * kc:(b + 1) * kc] = hi
-        own_lo[:, b * kc:(b + 1) * kc] = lo
-
-    for c in range(CHUNKS):
-        first = (c * kc) // block
-        span = pl.ds(c * kc, kc)
-        l_rows = jnp.concatenate([factor[:, :, b, :, span].reshape(block, kc) for b in range(first, chips)], axis=0)
+    for at, kc in spans:
+        hi, lo = halves(solved_buf[:, :, at:at + kc].reshape(pan * height, kc))
+        own_hi[:, at:at + kc] = hi
+        own_lo[:, at:at + kc] = lo
+
+    for c, (at, kc) in enumerate(spans):
+        first = at // block
+        l_rows = jnp.concatenate([factor[:, :, b, :, at:at + kc].reshape(block, kc) for b in range(first, chips)], axis=0)
         l_hi, l_lo = halves(l_rows)
         s_hi, s_lo = own_hi[:, first * block:], own_lo[:, first * block:]
         part = dot_nn(s_hi, l_hi) + (dot_nn(s_hi, l_lo) + dot_nn(s_lo, l_hi))
@@ -314,42 +323,58 @@
             q[c][h, col] = part[h]
         q_event(c, 0)
 
-    for c in range(CHUNKS):
-        row_event(c, 1)
-        if c > 0:
-            for d in range(1, far):
-                q_event(c - 1, d)
-    for d in range(2, chips - 1):
-        for c in range(CHUNKS):
-            row_event(c, d)
-            if d == 2 and c == 0:
-                for e in range(1, far):
-                    q_event(CHUNKS - 1, e)
-    for c in range(CHUNKS):
-        q_event(c, far)
-
-    over(0, slots, lambda t: slot_in(t).wait())
+    def q_relay(c):
+        for d in range(1, far):
+            q_event(c, d)
 
     def update(c):
+        kc = spans[c][1]
+
         def one(t):
-            left = q3[tiles[0, t]]
+            left = q3[tiles[0, t], :, 0:3 * kc]
             r_hi, r_lo = halves(sl[c][tiles[1, t]])
             right = jnp.concatenate([r_hi, r_lo, r_hi], axis=1)
             acc[t] = acc[t] - dot_nt(left, right)
         over(0, live, one)
 
-    for c in range(CHUNKS):
+    def complete(c):
+        q_event(c, far)
+        kc = spans[c][1]
         into = q3 if c < CHUNKS - 1 else q3_last
         for h in range(pan):
             hi, lo = halves(q[c][h].reshape(cols * height, kc))
             into[h, :, 0:kc] = hi
             into[h, :, kc:2 * kc] = hi
             into[h, :, 2 * kc:3 * kc] = lo
-        row_event(c, chips - 1)
+        for d in range(1, chips):
+            row_event(c, d, False)
         for i in range(PIECES[c]):
             over(0, chips, lambda src: row_sib(c, i, src, 1 - core).wait_recv())
-        if c < CHUNKS - 1:
-            update(c)
+
+    row_event(0, 1, True)
+    row_event(1, 1, True)
+    q_relay(0)
+    for d in range(2, chips - 1):
+        row_event(0, d, True)
+        if d == 2:
+            q_relay(1)
+        row_event(1, d, True)
+    own_send(3)
+    own_send(4)
+    q_relay(2)
+    for d in range(1, chips - 1):
+        row_event(2, d, True)
+        if d == 1:
+            q_relay(3)
+            q_relay(4)
+    for c in (3, 4):
+        for d in range(1, chips - 1):
+            row_event(c, d, True)
+    over(0, slots, lambda t: slot_in(t).wait())
+    for c in range(CHUNKS - 1):
+        complete(c)
+        update(c)
+    complete(CHUNKS - 1)
 
     factor_drain()
     for c in range(CHUNKS):
@@ -358,42 +383,42 @@
 
 
 def finish_kernel(rows, solved_buf, acc, q3, right_tiles, tiles, solved, updated,
-                  solved_stage, stage, solved_sem, out_sem):
+                  stage, solved_sem, rest_sem, out_sem):
     slots = acc.shape[0]
     live = live_slots(lax.axis_index("row"), rows, slots)
-    solved_copy = pltpu.make_async_copy(solved_stage, solved, solved_sem)
+    solved_copy = pltpu.make_async_copy(solved_buf, solved, solved_sem)
+
+    def rest_out(t):
+        return pltpu.make_async_copy(acc.at[t], updated.at[t], rest_sem.at[t])
 
     def slot_out(t):
         at = lax.rem(t, STAGES)
         return pltpu.make_async_copy(stage.at[at], updated.at[t], out_sem.at[at])
 
-    def staged(value):
-        def one(t):
-            @pl.when(t >= STAGES)
-            def _():
-                slot_out(t - STAGES).wait()
-
-            stage[lax.rem(t, STAGES)] = value(t)
-            slot_out(t).start()
-        return one
-
-    def touched(t):
+    over(live, slots, lambda t: rest_out(t).start())
+    solved_copy.start()
+
+    def one(t):
+        @pl.when(t >= STAGES)
+        def _():
+            slot_out(t - STAGES).wait()
+
         r_hi, r_lo = halves(right_tiles[tiles[1, t]])
         right = jnp.concatenate([r_hi, r_lo, r_hi], axis=1)
-        return acc[t] - dot_nt(q3[tiles[0, t]], right)
-
-    over(0, live, staged(touched))
-    over(live, slots, staged(lambda t: acc[t]))
-    solved_stage[...] = solved_buf[...]
-    solved_copy.start()
-    over(slots - STAGES, slots, lambda t: slot_out(t).wait())
+        stage[lax.rem(t, STAGES)] = acc[t] - dot_nt(q3[tiles[0, t]], right)
+        slot_out(t).start()
+
+    over(0, live, one)
+    over(live, slots, lambda t: rest_out(t).wait())
+    over(live - STAGES, live, lambda t: slot_out(t).wait())
     solved_copy.wait()
 
 
 def per_device(rows, cols, pivot_inverse, panel, trailing, tile_list):
     pan, height, order = panel.shape
     slots, _, width = trailing.shape
-    chips, kc = rows // 2, order // CHUNKS
+    chips = rows // 2
+    widths = [kc for _, kc in chunk_spans(order)]
     share = pivot_inverse.shape[0] // cols
     most = max(PIECES)
     dma = pltpu.SemaphoreType.DMA
@@ -406,18 +431,18 @@
         out_shape=(
             pltpu.VMEM(panel.shape, f32),
             pltpu.VMEM(trailing.shape, f32),
-            pltpu.VMEM((pan, cols * height, 3 * kc), bf16),
-            pltpu.VMEM((rows * pan, height, kc), f32),
+            pltpu.VMEM((pan, cols * height, 3 * widths[-1]), bf16),
+            pltpu.VMEM((rows * pan, height, widths[-1]), f32),
         ),
         in_specs=[anywhere, anywhere, anywhere, scalar],
         out_specs=(vector,) * 4,
         scratch_shapes=[
-            [pltpu.VMEM((rows * pan, height, kc), f32) for _ in range(CHUNKS - 1)],
-            [pltpu.VMEM((pan, cols, height, kc), f32) for _ in range(CHUNKS)],
+            [pltpu.VMEM((rows * pan, height, kc), f32) for kc in widths[:-1]],
+            [pltpu.VMEM((pan, cols, height, kc), f32) for kc in widths],
             pltpu.VMEM((2, cols, chips, share, order), f32),
             pltpu.VMEM((pan * height, order), bf16),
             pltpu.VMEM((pan * height, order), bf16),
-            pltpu.VMEM((pan, cols * height, 3 * kc), bf16),
+            pltpu.VMEM((pan, cols * height, 3 * max(widths)), bf16),
             dma((CHUNKS + 1,)),
             dma((slots,)),
             dma((chips,)),
@@ -434,7 +459,7 @@
             dma((CHUNKS, 2, cols, pan)),
         ],
         compiler_params=pltpu.CompilerParams(
-            collective_id=0, has_side_effects=True, vmem_limit_bytes=34 * 1024 * 1024
+            collective_id=0, has_side_effects=True, vmem_limit_bytes=36 * 1024 * 1024
         ),
     )(pivot_inverse, panel, trailing, tiles)
     carried = [pltpu.with_memory_space_constraint(x, pltpu.VMEM) for x in carried]
@@ -447,12 +472,12 @@
         in_specs=[vector, vector, vector, vector, scalar],
         out_specs=(anywhere, anywhere),
         scratch_shapes=[
-            pltpu.VMEM(panel.shape, f32),
             pltpu.VMEM((STAGES, order, width), f32),
             dma(()),
+            dma((slots,)),
             dma((STAGES,)),
         ],
-        compiler_params=pltpu.CompilerParams(vmem_limit_bytes=34 * 1024 * 1024),
+        compiler_params=pltpu.CompilerParams(vmem_limit_bytes=36 * 1024 * 1024),
     )(*carried, tiles)
 
 

time: 174 us -> 168 us (0.966)
  Pallas kernels: 173 us -> 167 us
    pallas_call x1, Pallas kernels: 14.7 us -> 11.3 us  [per_device(): pl.pallas_call(functools.partial(finish_kernel, rows), out_shape=(jax.Sha...]
    pallas_call x1, Pallas kernels: 159 us -> 155 us  [per_device(): pl.pallas_call(functools.partial(gather_kernel, rows, cols), out_shape=(p...]
where the time goes in v2:
time: 168 us; the launch traced here: 167 us
  Pallas kernels  167 us (99%)
    pallas_call x1, Pallas kernels, per_device(): pl.pallas_call(functools.partial(gather_kernel, rows, cols), out_shape=(p...  155 us
    pallas_call x1, Pallas kernels, per_device(): pl.pallas_call(functools.partial(finish_kernel, rows), out_shape=(jax.Sha...  11.3 us

profile of v2, /device:TPU:27, one launch (start us, length us, event | category | flops | bytes accessed | tf_op | source)
XLA Modules:
  0.0 167.3 jit_solution(18246635009967448773)
XLA Ops:
  0.6 155.4 %shard_map.59 = (f32[2,256,1024]{2,1,0:T(8,128)S(1)}, f32[20,1024,256]{2,1,0:T(8,128)S(1)}, bf16[2,1024,384]{2,1,0:T(8,128)(2,1)S(1)}, f32[16,256,128]{2,1,0:T(8,128)S(1)}) custom-call(f32[128,1024]{1,0:T(8,128)} %pivot.1, f32[2,256,1024]{2,1,0:T(8,128)} %panel.1, f32[20,1024,256]{2,1,0:T(8,128)} %trailing.1, s32[2,20]{1,0:T(2,128)} %bitcast.1), custom_call_target="tpu_custom_call" | custom-call | tf_op jit(solution)/shard_map/pallas_call | solution.py:429
  156.0 11.3 %shard_map.60 = (f32[2,256,1024]{2,1,0:T(8,128)}, f32[20,1024,256]{2,1,0:T(8,128)}) custom-call(f32[2,256,1024]{2,1,0:T(8,128)S(1)} %get-tuple-element.6.solved_buf, f32[20,1024,256]{2,1,0:T(8,128)S(1)} %get-tuple-element.7.acc, bf16[2,1024,384]{2,1,0:T(8,128)(2,1)S(1)} %get-tuple-element.8.q3, f32[16,256,128]{2,1,0:T(8,128)S(1)} %get-tuple-element.9.right_tiles, ...), custom_call_target="tpu_custom_call" | custom-call | tf_op jit(solution)/shard_map/pallas_call | solution.py:466

commit v3 on v2

--- a/solution.py
+++ b/solution.py
@@ -359,19 +359,31 @@
         if d == 2:
             q_relay(1)
         row_event(1, d, True)
-    own_send(3)
-    own_send(4)
     q_relay(2)
     for d in range(1, chips - 1):
         row_event(2, d, True)
-        if d == 1:
-            q_relay(3)
-            q_relay(4)
-    for c in (3, 4):
-        for d in range(1, chips - 1):
-            row_event(c, d, True)
+    middle = has_above & has_below
+    own_send(3)
+
+    @pl.when(~middle)
+    def _():
+        own_send(4)
+
+    q_relay(3)
+    q_relay(4)
+    for d in range(1, chips - 1):
+        row_event(3, d, True)
     over(0, slots, lambda t: slot_in(t).wait())
-    for c in range(CHUNKS - 1):
+    complete(0)
+    update(0)
+
+    @pl.when(middle)
+    def _():
+        own_send(4)
+
+    for d in range(1, chips - 1):
+        row_event(4, d, True)
+    for c in range(1, CHUNKS - 1):
         complete(c)
         update(c)
     complete(CHUNKS - 1)

time: 168 us -> 166 us (0.988)
  the two profiles are of different devices: /device:TPU:27 before, /device:TPU:16 now
where the time goes in v3:
time: 166 us; the launch traced here: 165 us
  Pallas kernels  165 us (99%)
    pallas_call x1, Pallas kernels, per_device(): pl.pallas_call(functools.partial(gather_kernel, rows, cols), out_shape=(p...  153 us
    pallas_call x1, Pallas kernels, per_device(): pl.pallas_call(functools.partial(finish_kernel, rows), out_shape=(jax.Sha...  11.3 us

profile of v3, /device:TPU:16, one launch (start us, length us, event | category | flops | bytes accessed | tf_op | source)
XLA Modules:
  0.0 165.3 jit_solution(8501316170480494083)
XLA Ops:
  0.6 153.4 %shard_map.59 = (f32[2,256,1024]{2,1,0:T(8,128)S(1)}, f32[20,1024,256]{2,1,0:T(8,128)S(1)}, bf16[2,1024,384]{2,1,0:T(8,128)(2,1)S(1)}, f32[16,256,128]{2,1,0:T(8,128)S(1)}) custom-call(f32[128,1024]{1,0:T(8,128)} %pivot.1, f32[2,256,1024]{2,1,0:T(8,128)} %panel.1, f32[20,1024,256]{2,1,0:T(8,128)} %trailing.1, s32[2,20]{1,0:T(2,128)} %bitcast.1), custom_call_target="tpu_custom_call" | custom-call | tf_op jit(solution)/shard_map/pallas_call | solution.py:441
  154.0 11.3 %shard_map.60 = (f32[2,256,1024]{2,1,0:T(8,128)}, f32[20,1024,256]{2,1,0:T(8,128)}) custom-call(f32[2,256,1024]{2,1,0:T(8,128)S(1)} %get-tuple-element.6.solved_buf, f32[20,1024,256]{2,1,0:T(8,128)S(1)} %get-tuple-element.7.acc, bf16[2,1024,384]{2,1,0:T(8,128)(2,1)S(1)} %get-tuple-element.8.q3, f32[16,256,128]{2,1,0:T(8,128)S(1)} %get-tuple-element.9.right_tiles, ...), custom_call_target="tpu_custom_call" | custom-call | tf_op jit(solution)/shard_map/pallas_call | solution.py:478
